TPU v7x, 128 devices: a whole 4x4x4 slice. The times are simulated.
128 devices in a mesh: dp: 16 (over z_hi, y, core), ctx: 8 (over x, z_lo).
Axes of the slice: x: 4, y: 4, z: 4 (z_hi: 2, z_lo: 2; z = z_hi * 2 + z_lo), core: 2. Of those that a mesh axis runs over, the one named last changes fastest.
Arguments:
- hidden: bfloat16 [16, 3072, 8192], P('dp', 'ctx'), may hold values from -6 to 6
- queries: bfloat16 [16, 3072, 4096], P('dp', 'ctx'), may hold values from -136 to 136
- weights_old: float32 [8192, 1024], P(('dp', 'ctx')), may hold values from -0.0625 to 0.0625
- gradient_old: float32 [8192, 1024], P(('dp', 'ctx')), may hold values from -6 to 6
- first_old: float32 [8192, 1024], P(('dp', 'ctx')), may hold values from -4 to 4
- second_old: float32 [8192, 1024], P(('dp', 'ctx')), may hold values from 0.25 to 4
- old_owner: int32 [128], replicated, may hold values from 0 to 127, each once
- new_owner: int32 [128], replicated, may hold values from 0 to 127, each once
- offsets: int32 [16, 8, 2], P('dp'), may hold values from 0 to 2880, as said below
Outputs:
- weights_new: float32 [1024, 8192], P(('dp', 'ctx'))
- first_new: float32 [1024, 8192], P(('dp', 'ctx'))
- second_new: float32 [1024, 8192], P(('dp', 'ctx'))
- attended: bfloat16 [16, 3072, 4096], P('dp', 'ctx')
Inputs may be any that keep to these rules, and one draw needn't show every extreme that they name: `offsets`: for sequence b and ctx index c the two entries are p * 192 and (15 - p) * 192, where p runs over a permutation of the ctx indices drawn for each sequence. `old_owner`: each block index appears once. `new_owner`: each block index appears once.
All inputs are finite; a program needn't handle non-finite values.
Results may differ from a plain program's by a relative error of at most 0.0055.
The roundings to bfloat16 on the way count: a program that leaves them out, or rounds other values in their place, can miss the bound.
Values may be sent and summed in bfloat16 or wider, within the bound.
No kernel may reach another device: no remote copies, remote signals or barrier semaphores. Data moves between devices by JAX's collectives and lax.ppermute only.
A program may use at most 320 MiB of HBM per device.

v0:
```python
import math
import jax
import jax.numpy as jnp
from jax import lax
from jax.sharding import PartitionSpec as P

HEAD = 128
KV_HEADS = 4
Q_HEADS = 32
learn_rate = 0.0003
beta_one = 0.9
beta_two = 0.95
adam_eps = 1e-08
decay_rate = 0.1
step_number = 1000
corr_one = 1.0 - beta_one**step_number
corr_two = 1.0 - beta_two**step_number
rope_base = 500000.0


def in_blocks(value, dim, peers):
    before, after = (value.shape[:dim], value.shape[dim + 1 :])
    return jnp.moveaxis(value.reshape(*before, peers, -1, *after), dim, 0)


def joined_along(tiles, dim):
    dims = list(tiles.shape[1:])
    dims[dim] *= tiles.shape[0]
    return jnp.moveaxis(tiles, 0, dim).reshape(dims)


def one_exchange(value, axis, axes, splits, concats):
    sizes = [lax.axis_size(a) for a in axes]
    tiles = in_blocks(value, splits[0], sizes[0])
    tiles = jnp.moveaxis(in_blocks(tiles, splits[1] + 1, sizes[1]), 0, 1)
    inside = tiles.shape[2:]
    tiles = tiles.reshape(-1, *inside)
    tiles = lax.all_to_all(tiles, axis, split_axis=0, concat_axis=0, tiled=True)
    tiles = joined_along(tiles.reshape(*sizes, *inside), concats[0] + 1)
    return joined_along(tiles, concats[1])


def adam_step(weights, gradient, first_mom, second_mom):
    first_next = beta_one * first_mom + (1.0 - beta_one) * gradient
    second_next = beta_two * second_mom + (1.0 - beta_two) * gradient * gradient
    direction = first_next / corr_one / (jnp.sqrt(second_next / corr_two) + adam_eps)
    weights_next = weights - learn_rate * (direction + decay_rate * weights)
    return (weights_next, first_next, second_next)


def rotate_keys(key_heads, positions):
    head_dim = key_heads.shape[-1]
    half_dim = head_dim // 2
    exponent = jnp.arange(half_dim, dtype=jnp.float32) * (2.0 / head_dim)
    inv_freq = jnp.power(rope_base, -exponent)
    angles = positions.astype(jnp.float32)[..., None] * inv_freq
    cosine = jnp.cos(angles)[..., None, :]
    sine_part = jnp.sin(angles)[..., None, :]
    first_half = key_heads[..., :half_dim]
    second_half = key_heads[..., half_dim:]
    return jnp.concatenate(
        [
            first_half * cosine - second_half * sine_part,
            second_half * cosine + first_half * sine_part,
        ],
        axis=-1,
    )


def invert(owners):
    devices = owners.shape[0]
    return jnp.zeros((devices,), jnp.int32).at[owners].set(jnp.arange(devices, dtype=jnp.int32))


def relocate(stacked, new_owner, old_owner):
    states_count, row_count, proj_width = stacked.shape
    devices = new_owner.shape[0]
    col_count = proj_width // devices
    outgoing = stacked.reshape(states_count, row_count, devices, col_count).transpose(2, 0, 3, 1)
    outgoing = jnp.take(outgoing, new_owner, axis=0)
    grid_form = outgoing.reshape((lax.axis_size("dp"), lax.axis_size("ctx")) + outgoing.shape[1:])
    incoming = one_exchange(grid_form, ("dp", "ctx"), ("dp", "ctx"), (0, 1), (0, 1)).reshape(
        outgoing.shape
    )
    ordered = jnp.take(incoming, invert(old_owner), axis=0)
    return ordered.transpose(1, 2, 0, 3).reshape(states_count, col_count, devices * row_count)


def shards(
    hidden, queries, weights_old, gradient_old, first_old, second_old, old_owner, new_owner, offsets
):
    devices = old_owner.shape[0]
    row_count, proj_width = weights_old.shape
    tok_rows = hidden.shape[1]
    half_tok = tok_rows // 2
    model_width = hidden.shape[2]
    head_dim = HEAD
    kv_heads = KV_HEADS
    groups = Q_HEADS // KV_HEADS
    key_width = kv_heads * head_dim
    tokens_flat = hidden[0]
    updated = adam_step(weights_old, gradient_old, first_old, second_old)
    moved = relocate(jnp.stack(updated), new_owner, old_owner)
    weights_new, first_new, second_new = (moved[0], moved[1], moved[2])
    weights_next = adam_step(weights_old, gradient_old, first_old, second_old)[0]
    copies = weights_next.astype(jnp.bfloat16)
    permuted = jnp.take(
        tokens_flat.reshape(tok_rows, devices, row_count), old_owner, axis=1
    ).reshape(tok_rows, model_width)
    segment = lax.all_gather(copies, ("dp", "ctx"), axis=0, tiled=True)
    columns = lax.slice_in_dim(permuted, 0, segment.shape[0], axis=1)
    projected = jnp.zeros((tok_rows, proj_width), jnp.float32) + jnp.dot(
        columns, segment, preferred_element_type=jnp.float32
    )
    offset_table = offsets[0]
    ctx_count = offset_table.shape[0]
    flat_table = offset_table.reshape(2 * ctx_count)
    slot_ids = jnp.arange(2 * ctx_count, dtype=jnp.int32)

    def lookup(rows_global):
        device_of = rows_global // tok_rows
        local_row = rows_global % tok_rows
        slot_index = device_of * 2 + local_row // half_tok
        picked = slot_index[:, None] == slot_ids[None, :]
        return jnp.sum(jnp.where(picked, flat_table[None, :], 0), axis=1) + local_row % half_tok

    own_rows = lax.axis_index("ctx") * tok_rows + jnp.arange(tok_rows, dtype=jnp.int32)
    query_pos = lookup(own_rows)
    key_heads = projected[:, :key_width].reshape(tok_rows, kv_heads, head_dim)
    key_rows = rotate_keys(key_heads, query_pos).reshape(tok_rows, key_width).astype(jnp.bfloat16)
    value_rows = projected[:, key_width:].astype(jnp.bfloat16)
    query_heads = queries[0].reshape(tok_rows, kv_heads, groups, head_dim)
    inv_root = 1.0 / math.sqrt(head_dim)
    best_score = jnp.full((kv_heads, groups, tok_rows), -1e30, jnp.float32)
    key_block = lax.all_gather(key_rows, "ctx", axis=0, tiled=True)
    value_block = lax.all_gather(value_rows, "ctx", axis=0, tiled=True)
    block_rows = key_block.shape[0]
    key_pos = lookup(jnp.arange(block_rows, dtype=jnp.int32))
    key_split = key_block.reshape(block_rows, kv_heads, head_dim)
    scores = (
        jnp.einsum("tkgd,nkd->kgtn", query_heads, key_split, preferred_element_type=jnp.float32)
        * inv_root
    )
    visible = key_pos[None, None, None, :] <= query_pos[None, None, :, None]
    masked = jnp.where(visible, scores, -1e30)
    best_next = jnp.maximum(best_score, jnp.max(masked, axis=3))
    exp_terms = jnp.where(visible, jnp.exp(masked - best_next[..., None]), 0.0)
    totals_next = jnp.sum(exp_terms, axis=3)
    value_split = value_block.reshape(block_rows, kv_heads, head_dim)
    increment = jnp.einsum(
        "kgtn,nkd->tkgd",
        exp_terms.astype(jnp.bfloat16),
        value_split,
        preferred_element_type=jnp.float32,
    )
    result = increment / jnp.transpose(totals_next, (2, 0, 1))[..., None]
    attended = result.reshape(1, tok_rows, Q_HEADS * head_dim).astype(jnp.bfloat16)
    return (weights_new, first_new, second_new, attended)


def solution(mesh):
    in_specs = (
        P("dp", "ctx", None),
        P("dp", "ctx", None),
        P(("dp", "ctx"), None),
        P(("dp", "ctx"), None),
        P(("dp", "ctx"), None),
        P(("dp", "ctx"), None),
        P(),
        P(),
        P("dp", None, None),
    )
    out_specs = (
        P(("dp", "ctx"), None),
        P(("dp", "ctx"), None),
        P(("dp", "ctx"), None),
        P("dp", "ctx", None),
    )
    return jax.shard_map(shards, mesh=mesh, in_specs=in_specs, out_specs=out_specs, check_vma=False)
```

profile of v0, /device:TPU:4, one launch (start us, length us, event | category | flops | bytes accessed | tf_op | source)
XLA Modules:
  0.0 606.7 jit_solution(16304854576319501626)
XLA Ops:
  7.2 2.0 fusion.45
  9.3 0.8 copy.64
  10.2 8.6 %copy.63 = bf16[1,384,8192]{1,2,0:T(8,128)(2,1)} copy(bf16[1,384,8192]{2,1,0:T(8,128)(2,1)} %param.11) | data formatting | bytes 12582912 | tf_op args[0]
  18.8 0.1 broadcast_in_dim.86
  18.9 0.1 broadcast_in_dim.87
  19.0 6.8 %gather_fusion = bf16[128,384,64]{1,2,0:T(8,128)(2,1)} fusion(bf16[384,128,64]{0,2,1:T(8,128)(2,1)} %bitcast.75, s32[1024]{0:T(1024)S(1)} %pad_clamp_fusion), kind=kCustom, calls=%fused_computation.2 | custom fusion | bytes 12583424 | tf_op jit(solution)/shard_map/jit(_take)/gather | solution.py:107
  25.9 0.1 select_reduce_fusion.1
  26.0 0.8 multiply_cosine_fusion
  26.8 8.0 %bitcast_select_fusion.1 = bf16[384,8192]{0,1:T(8,128)(2,1)} fusion(bf16[128,384,64]{1,2,0:T(8,128)(2,1)} %gather_fusion, pred[8192]{0:T(1024)(128)(4,1)S(1)} %broadcast_in_dim.87), kind=kLoop, calls=%fused_computation.11 | loop fusion | flops 3145728 | bytes 12591104 | tf_op jit(solution)/shard_map/jit(_take)/select_n | solution.py:107
  34.8 299.3 %all-gather.4.cloned.1.call-done = bf16[8192,1024]{1,0:T(8,128)(2,1)} async-done(((bf16[64,1024]{1,0:T(8,128)(2,1)}), bf16[8192,1024]{1,0:T(8,128)(2,1)}) %all-gather.4.cloned.1.call-update) | async-done | bytes 16777232 | tf_op jit(solution)/shard_map/all_gather | solution.py:110
  334.1 12.2 %fusion.48 = f32[384,1024]{1,0:T(8,128)S(1)} fusion(bf16[384,8192]{0,1:T(8,128)(2,1)} %bitcast_select_fusion.1, bf16[8192,1024]{1,0:T(8,128)(2,1)} %all-gather.4.cloned.1.call-done), kind=kOutput, calls=%fused_computation.93 | convolution fusion | flops 6442450944 | bytes 24641536 | tf_op jit(solution)/shard_map/dot_general | solution.py:112
  346.3 1.2 copy-done
  347.5 0.3 reshape.259
  347.8 0.6 subtract_convert_fusion
  348.4 0.5 pad_maximum_fusion
  349.0 1.0 copy.65
  350.0 0.2 copy.55
  350.2 0.2 copy.54
  350.4 0.2 copy.53
  350.7 0.1 maximum_bitcast_fusion
  350.8 0.8 gather_fusion.1
  351.6 0.2 select_bitcast_fusion.1
  351.8 1.9 reshape.305
  353.7 9.9 %all-to-all-start = ((f32[128,1,1536]{2,1,0:T(1,128)}), f32[128,1,1536]{2,1,0:T(1,128)S(1)}, u32[]{:S(2)}, u32[]{:S(2)}) async-start(f32[128,1,1536]{2,1,0:T(1,128)} %reshape.305), calls=%async_computation | async-start | bytes 1572864 | tf_op jit(solution)/shard_map/all_to_all | solution.py:38
  363.6 4.4 copy.77
  368.0 1.0 scatter_custom_fusion
  369.0 0.1 select_reduce_fusion
  369.2 2.4 broadcast_compare_fusion
  371.6 7.1 %all-to-all-done = f32[128,1,1536]{2,1,0:T(1,128)S(1)} async-done(((f32[128,1,1536]{2,1,0:T(1,128)}), f32[128,1,1536]{2,1,0:T(1,128)S(1)}, u32[]{:S(2)}, u32[]{:S(2)}) %all-to-all-start) | async-done | bytes 786464 | tf_op jit(solution)/shard_map/all_to_all | solution.py:38
  378.8 0.5 broadcast.364
  379.3 2.5 reduce
  381.8 0.3 reshape.306
  382.1 0.8 gather_fusion.2
  382.9 0.2 select_bitcast_fusion
  383.1 0.1 fusion.47
  383.3 0.1 copy.60
  383.4 0.9 squeeze.9
  384.3 0.1 copy.61
  384.4 0.9 squeeze.10
  385.2 0.1 copy.62
  385.3 0.9 squeeze.11
  386.2 1.9 slice.50
  388.2 42.9 %all-gather.8.cloned.1.call-done = bf16[3072,512]{0,1:T(8,128)(2,1)} async-done(((bf16[384,512]{0,1:T(8,128)(2,1)}), bf16[3072,512]{0,1:T(8,128)(2,1)}) %all-gather.8.cloned.1.call-update) | async-done | bytes 3145744 | tf_op jit(solution)/shard_map/all_gather | solution.py:135
  431.1 56.4 %fusion = (f32[4,8,384]{2,1,0:T(8,128)S(1)}, f32[4,3072,384,8]{2,1,3,0:T(8,128)}) fusion(pred[384,3072]{0,1:T(8,128)(4,1)S(1)} %copy-done.1, bf16[3072,4,128,1]{0,2,3,1:T(8,128)(2,1)} %bitcast.86, bf16[384,4,8,128]{3,2,1,0:T(8,128)(2,1)} %bitcast.78), kind=kOutput, calls=%fused_computation.6 | convolution fusion | flops 9776910336 | bytes 158515200 | tf_op jit(solution)/shard_map/tkgd,nkd->kgtn/dot_general | solution.py:141
  487.5 46.2 %fusion.1 = f32[4,8,384]{2,1,0:T(8,128)S(1)} fusion(f32[4,3072,384,8]{2,1,3,0:T(8,128)} %get-tuple-element.35, f32[4,8,384]{2,1,0:T(8,128)S(1)} %broadcast_maximum_fusion, pred[384,3072]{0,1:T(8,128)(4,1)S(1)} %copy-done.1), kind=kLoop, calls=%fused_computation.7 | loop fusion | flops 188731392 | bytes 152272896 | tf_op jit(solution)/shard_map/reduce_sum | solution.py:148
  533.8 4.9 copy.74
  538.6 56.9 %fusion.6 = bf16[384,4,8,128]{0,3,2,1:T(8,128)(2,1)} fusion(f32[384,4,8]{0,2,1:T(8,128)S(1)} %bitcast.85, bf16[3072,4,128,1]{0,2,3,1:T(8,128)(2,1)} %bitcast.79, f32[4,3072,384,8]{2,1,3,0:T(8,128)} %get-tuple-element.35, f32[4,8,384]{2,1,0:T(8,128)S(1)} %broadcast_maximum_fusion, pred[384,3072]{0,1:T(8,128)(4,1)S(1)} %copy-done.1), kind=kOutput, calls=%fused_computation.13 | convolution fusion | flops 9855565824 | bytes 158564352 | tf_op jit(solution)/shard_map/kgtn,nkd->tkgd/dot_general | solution.py:150
  595.6 4.6 copy.70
  (32 shorter events, 0.5 us)
Async XLA Ops:
  7.2 326.9 %all-gather.4.cloned.1.call-start = ((), (), s32[]{:S(2)}) async-start(), calls=%async_computation.1 | async-start | bytes 16908288 | tf_op jit(solution)/shard_map/all_gather | solution.py:110
  9.3 421.8 %all-gather.8.cloned.1.call-start = ((), (), s32[]{:S(2)}) async-start(), calls=%async_computation.3 | async-start | bytes 3538944 | tf_op jit(solution)/shard_map/all_gather | solution.py:135
  10.2 8.6 %copy-start.2 = (s32[128]{0:T(128)S(1)}, s32[128]{0:T(128)}, u32[]{:S(2)}) copy-start(s32[128]{0:T(128)} %param.17) | copy-start | bytes 1540
  346.3 1.2 copy-start
  347.5 3.1 copy-start.3
  353.7 25.1 %all-to-all-start = ((f32[128,1,1536]{2,1,0:T(1,128)}), f32[128,1,1536]{2,1,0:T(1,128)S(1)}, u32[]{:S(2)}, u32[]{:S(2)}) async-start(f32[128,1,1536]{2,1,0:T(1,128)} %reshape.305), calls=%async_computation | async-start | bytes 1572864 | tf_op jit(solution)/shard_map/all_to_all | solution.py:38
  363.6 170.2 %all-gather.6.cloned.1.call-start = ((), (), s32[]{:S(2)}) async-start(), calls=%async_computation.2 | async-start | bytes 3538944 | tf_op jit(solution)/shard_map/all_gather | solution.py:136
  383.1 48.0 %copy-start.1 = (pred[384,3072]{0,1:T(8,128)(4,1)S(1)}, pred[384,3072]{0,1:T(8,128)(4,1)}, u32[]{:S(2)}) copy-start(pred[384,3072]{0,1:T(8,128)(4,1)} %broadcast_compare_fusion) | copy-start | bytes 3538948
Sparse Core Ops, SparseCore 0:
  10.2 323.8 all-gather.3
  350.1 80.9 all-gather.7
  432.8 70.5 all-gather.5
where the time goes:
time: 608 us; the launch traced here: 607 us
  waiting for transfers between devices  349 us (57%)
  matrix products  125 us (21%)
  other arithmetic  64 us (11%)
  local copies, waits for them, and re-layouts  43.7 us (7%)
  between operations  14.1 us (2%)
  starting transfers between devices  10 us (2%)
    all_gather x1, waiting for transfers between devices, shards(): segment = lax.all_gather(copies, ('dp', 'ctx'), axis=0, tiled=True)  299 us
    dot_general x1, matrix products, shards(): jnp.einsum('kgtn,nkd->tkgd', exp_terms.astype(jnp.bfloat16), value_split,...  56.9 us
    dot_general x1, matrix products, shards(): jnp.einsum('tkgd,nkd->kgtn', query_heads, key_split, preferred_element_ty...  56.4 us
    reduce_sum x1, other arithmetic, shards(): totals_next = jnp.sum(exp_terms, axis=3)  46.2 us
    all_gather x1, waiting for transfers between devices, shards(): key_block = lax.all_gather(key_rows, 'ctx', axis=0, tiled=True)  42.9 us
    unnamed x14, local copies, waits for them, and re-layouts  21.8 us
    dot_general x1, matrix products, shards(): jnp.dot(columns, segment, preferred_element_type=jnp.float32)  12.2 us
  transfers between devices with their start and end apart: 4, of which 3 were waited for; matrix products, arithmetic and copies ran while one was open for 25% of the time, Pallas kernels for 0%

commit v1 on v0

--- a/solution.py
+++ b/solution.py
@@ -132,8 +132,13 @@
     query_heads = queries[0].reshape(tok_rows, kv_heads, groups, head_dim)
     inv_root = 1.0 / math.sqrt(head_dim)
     best_score = jnp.full((kv_heads, groups, tok_rows), -1e30, jnp.float32)
-    key_block = lax.all_gather(key_rows, "ctx", axis=0, tiled=True)
-    value_block = lax.all_gather(value_rows, "ctx", axis=0, tiled=True)
+
+    def _detail_islands(x_local, t0, axis_key):
+        value_now = jnp.concatenate([x_local, t0], 1)
+        main = lax.all_gather(value_now, axis_key, tiled=True, axis=0)
+        return jnp.split(main, [x_local.shape[1]], 1)
+
+    key_block, value_block = _detail_islands(key_rows, value_rows, "ctx")
     block_rows = key_block.shape[0]
     key_pos = lookup(jnp.arange(block_rows, dtype=jnp.int32))
     key_split = key_block.reshape(block_rows, kv_heads, head_dim)

time: 608 us -> 674 us (1.11)
  waiting for transfers between devices: 349 us -> 409 us
    all_gather x2 -> x1, waiting for transfers between devices: 42.9 us -> 96.8 us  [_detail_islands(): main = lax.all_gather(value_now, axis_key, tiled=True, axis=0)]
    unnamed x14 -> x13, local copies, waits for them, and re-layouts: 21.8 us -> 20.7 us
  transfers between devices with their start and end apart: 4 -> 3, of which waited for: 3 -> 3; matrix products, arithmetic and copies ran while one was open for 25% -> 7% of each run, Pallas kernels for 0% -> 0%
where the time goes in v1:
time: 674 us; the launch traced here: 672 us
  waiting for transfers between devices  409 us (61%)
  matrix products  125 us (19%)
  other arithmetic  65.7 us (10%)
  local copies, waits for them, and re-layouts  47.7 us (7%)
  between operations  14.3 us (2%)
  starting transfers between devices  9.99 us (1%)
    all_gather x1, waiting for transfers between devices, shards(): segment = lax.all_gather(copies, ('dp', 'ctx'), axis=0, tiled=True)  299 us
    all_gather x1, waiting for transfers between devices, _detail_islands(): main = lax.all_gather(value_now, axis_key, tiled=True, axis=0)  96.8 us
    dot_general x1, matrix products, shards(): jnp.einsum('kgtn,nkd->tkgd', exp_terms.astype(jnp.bfloat16), value_split,...  57.1 us
    dot_general x1, matrix products, shards(): jnp.einsum('tkgd,nkd->kgtn', query_heads, key_split, preferred_element_ty...  55.6 us
    reduce_sum x1, other arithmetic, shards(): totals_next = jnp.sum(exp_terms, axis=3)  46.5 us
    unnamed x13, local copies, waits for them, and re-layouts  20.7 us
    all_to_all x1, waiting for transfers between devices, one_exchange(): tiles = lax.all_to_all(tiles, axis, split_axis=0, concat_axis=0, tiled=True)  13.6 us
  transfers between devices with their start and end apart: 3, of which 3 were waited for; matrix products, arithmetic and copies ran while one was open for 7% of the time, Pallas kernels for 0%

profile of v1, /device:TPU:4, one launch (start us, length us, event | category | flops | bytes accessed | tf_op | source)
XLA Modules:
  0.0 671.6 jit_solution(3340102781258294426)
XLA Ops:
  7.2 2.0 fusion.46
  9.3 0.8 copy.63
  10.2 0.7 compare_and_fusion.2
  10.9 0.1 broadcast_in_dim.87
  11.0 8.6 %copy.62 = bf16[1,384,8192]{1,2,0:T(8,128)(2,1)} copy(bf16[1,384,8192]{2,1,0:T(8,128)(2,1)} %param.11) | data formatting | bytes 12582912 | tf_op args[0]
  19.7 6.9 %gather_fusion = bf16[128,384,64]{1,2,0:T(8,128)(2,1)} fusion(bf16[384,128,64]{0,2,1:T(8,128)(2,1)} %bitcast.74, s32[1024]{0:T(1024)S(1)} %pad_clamp_fusion), kind=kCustom, calls=%fused_computation.2 | custom fusion | bytes 12583424 | tf_op jit(solution)/shard_map/jit(_take)/gather | solution.py:107
  26.6 0.1 select_reduce_fusion.1
  26.7 0.8 multiply_cosine_fusion
  27.5 8.0 %bitcast_select_fusion.1 = bf16[384,8192]{0,1:T(8,128)(2,1)} fusion(bf16[128,384,64]{1,2,0:T(8,128)(2,1)} %gather_fusion, pred[8192]{0:T(1024)(128)(4,1)S(1)} %broadcast_in_dim.87), kind=kLoop, calls=%fused_computation.11 | loop fusion | flops 3145728 | bytes 12591104 | tf_op jit(solution)/shard_map/jit(_take)/select_n | solution.py:107
  35.5 298.6 %all-gather.3.cloned.1.call-done = bf16[8192,1024]{1,0:T(8,128)(2,1)} async-done(((bf16[64,1024]{1,0:T(8,128)(2,1)}), bf16[8192,1024]{1,0:T(8,128)(2,1)}) %all-gather.3.cloned.1.call-update) | async-done | bytes 16777232 | tf_op jit(solution)/shard_map/all_gather | solution.py:110
  334.1 12.2 %fusion.50 = f32[384,1024]{1,0:T(8,128)S(1)} fusion(bf16[384,8192]{0,1:T(8,128)(2,1)} %bitcast_select_fusion.1, bf16[8192,1024]{1,0:T(8,128)(2,1)} %all-gather.3.cloned.1.call-done), kind=kOutput, calls=%fused_computation.97 | convolution fusion | flops 6442450944 | bytes 24641536 | tf_op jit(solution)/shard_map/dot_general | solution.py:112
  346.4 0.3 reshape.258
  346.7 0.6 subtract_convert_fusion
  347.4 0.5 pad_maximum_fusion.1
  348.0 1.0 pad_maximum_fusion
  349.0 0.2 copy.52
  349.2 0.2 copy.53
  349.4 0.2 copy.54
  349.6 0.1 maximum_bitcast_fusion
  349.7 0.8 gather_fusion.1
  350.6 0.2 select_bitcast_fusion.1
  350.8 1.9 reshape.305
  352.6 9.9 %all-to-all-start = ((f32[128,1,1536]{2,1,0:T(1,128)}), f32[128,1,1536]{2,1,0:T(1,128)S(1)}, u32[]{:S(2)}, u32[]{:S(2)}) async-start(f32[128,1,1536]{2,1,0:T(1,128)} %reshape.305), calls=%async_computation | async-start | bytes 1572864 | tf_op jit(solution)/shard_map/all_to_all | solution.py:38
  362.5 4.4 copy.76
  366.9 1.2 scatter_custom_fusion
  368.1 0.1 select_reduce_fusion
  368.3 2.2 broadcast_compare_fusion
  370.5 13.6 %all-to-all-done = f32[128,1,1536]{2,1,0:T(1,128)S(1)} async-done(((f32[128,1,1536]{2,1,0:T(1,128)}), f32[128,1,1536]{2,1,0:T(1,128)S(1)}, u32[]{:S(2)}, u32[]{:S(2)}) %all-to-all-start) | async-done | bytes 786464 | tf_op jit(solution)/shard_map/all_to_all | solution.py:38
  384.1 0.5 broadcast.364
  384.6 2.5 reduce
  387.1 0.3 reshape.306
  387.5 0.8 gather_fusion.2
  388.3 0.2 select_bitcast_fusion
  388.5 0.1 fusion.49
  388.6 0.1 copy.61
  388.7 0.9 squeeze.11
  389.6 0.1 copy.60
  389.7 0.9 squeeze.10
  390.6 0.1 copy.59
  390.7 0.9 squeeze.9
  391.6 96.8 %all-gather.5.cloned.1.call-done = bf16[3072,1024]{1,0:T(8,128)(2,1)} async-done(((bf16[384,1024]{1,0:T(8,128)(2,1)}), bf16[3072,1024]{1,0:T(8,128)(2,1)}) %all-gather.5.cloned.1.call-update) | async-done | bytes 6291472 | tf_op jit(solution)/shard_map/all_gather | solution.py:138
  488.4 4.9 fusion.48
  493.3 4.7 copy.72
  498.0 3.0 reshape.260
  500.9 55.6 %fusion = (f32[4,8,384]{2,1,0:T(8,128)S(1)}, f32[4,3072,384,8]{2,1,3,0:T(8,128)}) fusion(pred[384,3072]{0,1:T(8,128)(4,1)} %broadcast_compare_fusion, bf16[384,4,8,128]{3,2,1,0:T(8,128)(2,1)} %bitcast.77, bf16[3072,4,128,1]{2,1,0,3:T(4,128)(2,1)} %bitcast.80), kind=kOutput, calls=%fused_computation.6 | convolution fusion | flops 9776910336 | bytes 158515200 | tf_op jit(solution)/shard_map/tkgd,nkd->kgtn/dot_general | solution.py:146
  556.6 46.5 %fusion.1 = f32[4,8,384]{2,1,0:T(8,128)S(1)} fusion(f32[4,3072,384,8]{2,1,3,0:T(8,128)} %get-tuple-element.37, f32[4,8,384]{2,1,0:T(8,128)S(1)} %broadcast_maximum_fusion, pred[384,3072]{0,1:T(8,128)(4,1)S(1)} %copy-done), kind=kLoop, calls=%fused_computation.7 | loop fusion | flops 188731392 | bytes 152272896 | tf_op jit(solution)/shard_map/reduce_sum | solution.py:153
  603.1 57.1 %fusion.6 = bf16[384,4,8,128]{0,3,2,1:T(8,128)(2,1)} fusion(f32[384,4,8]{0,2,1:T(8,128)S(1)} %bitcast.86, bf16[3072,4,128,1]{0,2,3,1:T(8,128)(2,1)} %bitcast.78, f32[4,3072,384,8]{2,1,3,0:T(8,128)} %get-tuple-element.37, f32[4,8,384]{2,1,0:T(8,128)S(1)} %broadcast_maximum_fusion, pred[384,3072]{0,1:T(8,128)(4,1)S(1)} %copy-done), kind=kOutput, calls=%fused_computation.13 | convolution fusion | flops 9855565824 | bytes 158564352 | tf_op jit(solution)/shard_map/kgtn,nkd->tkgd/dot_general | solution.py:155
  660.1 4.6 copy.68
  (30 shorter events, 0.6 us)
Async XLA Ops:
  7.2 326.9 %all-gather.3.cloned.1.call-start = ((), (), s32[]{:S(2)}) async-start(), calls=%async_computation.1 | async-start | bytes 16908288 | tf_op jit(solution)/shard_map/all_gather | solution.py:110
  9.3 479.1 %all-gather.5.cloned.1.call-start = ((), (), s32[]{:S(2)}) async-start(), calls=%async_computation.2 | async-start | bytes 7077888 | tf_op jit(solution)/shard_map/all_gather | solution.py:138
  11.0 8.7 %copy-start.1 = (s32[128]{0:T(128)S(1)}, s32[128]{0:T(128)}, u32[]{:S(2)}) copy-start(s32[128]{0:T(128)} %param.17) | copy-start | bytes 1540
  347.3 2.3 copy-start.2
  352.6 31.5 %all-to-all-start = ((f32[128,1,1536]{2,1,0:T(1,128)}), f32[128,1,1536]{2,1,0:T(1,128)S(1)}, u32[]{:S(2)}, u32[]{:S(2)}) async-start(f32[128,1,1536]{2,1,0:T(1,128)} %reshape.305), calls=%async_computation | async-start | bytes 1572864 | tf_op jit(solution)/shard_map/all_to_all | solution.py:38
  500.9 55.7 %copy-start = (pred[384,3072]{0,1:T(8,128)(4,1)S(1)}, pred[384,3072]{0,1:T(8,128)(4,1)}, u32[]{:S(2)}) copy-start(pred[384,3072]{0,1:T(8,128)(4,1)} %broadcast_compare_fusion) | copy-start | bytes 3538948
Sparse Core Ops, SparseCore 0:
  10.2 323.8 all-gather.2
  349.1 139.2 all-gather.4
